TPU v7x, 32 devices: a whole 2x2x4 slice. The times are simulated.
32 devices in a mesh: shot: 4 (over x, core), tile: 8 (over z, y).
Axes of the slice: x: 2, y: 2, z: 4, core: 2. Of those that a mesh axis runs over, the one named last changes fastest.
Arguments:
- adjoint_now: float32 [4, 64, 64, 128], P('shot', 'tile'), may hold values from -6 to 6
- adjoint_prev: float32 [4, 64, 64, 128], P('shot', 'tile'), may hold values from -6 to 6
- costates: float32 [4, 6, 64, 64, 128], P('shot', None, 'tile'), may hold values from -6 to 6
- modulus: float32 [64, 64, 128], P('tile'), may hold values from 0.04 to 0.2
- relaxation: float32 [64, 64, 128], P('tile'), may hold values from 0.1 to 0.6
- absorb_mask: int32 [64, 64, 128], P('tile'), may hold values from 0 to 1, as said below
- relax_rates: float32 [6], replicated, may hold values from 0.02 to 2
- mech_weights: float32 [6], replicated, may hold values from 0.1 to 1
- forward_lap: bfloat16 [4, 6, 64, 64, 128], P('shot', None, 'tile'), may hold values from -0.59765625 to 0.59765625
- recv_cells: int32 [4, 512], P('shot'), may hold values from 0 to 524287
- enc_signs: int32 [4, 8], P('shot'), may hold values from -1 to 1, as said below
- residuals: float32 [4, 8, 6, 512], P('shot'), may hold values from -6 to 6
Outputs:
- adjoint_out: float32 [4, 64, 64, 128], P('shot', 'tile')
- grad_modulus: float32 [64, 64, 128], P('tile', 'shot')
- grad_relax: float32 [64, 64, 128], P('tile', 'shot')
Inputs may be any that keep to these rules, and one draw needn't show every extreme that they name: absorb_mask is 1 in layers along all six faces of the grid, each 1 to 8 cells thick and at most a quarter of the grid's extent, and 0 inside. `enc_signs`: each entry is -1 or +1.
All inputs are finite; a program needn't handle non-finite values.
Results may differ from a plain program's by a relative error of at most 0.00055.
Values sent between devices are 32-bit elements; how exact they have to be, the bound alone decides.
A program may use at most 64 MiB of HBM per device.

v0:
```python
import jax
import jax.numpy as jnp
from jax import lax
from jax.sharding import PartitionSpec as P

STEPS = 6


coeffs = (-205.0 / 72.0, 8.0 / 5.0, -1.0 / 5.0, 8.0 / 315.0, -1.0 / 560.0)
damping = 0.2


def with_halo(x, sides, width):
    for axis, dim in sides:
        devices, length = (lax.axis_size(axis), x.shape[dim])
        up = [(i, (i + 1) % devices) for i in range(devices - 1)]
        down = [(j, i) for i, j in up]
        last = lax.slice_in_dim(x, length - width, length, axis=dim)
        leading = lax.slice_in_dim(x, 0, width, axis=dim)
        before = lax.ppermute(last, axis, up)
        after = lax.ppermute(leading, axis, down)
        x = jnp.concatenate([before, x, after], axis=dim)
    return x


def laplace_cross(field):
    tile_rows, tile_cols, tile_depth = field.shape
    padded = jnp.pad(field, ((0, 0), (4, 4), (4, 4)))
    result = 2.0 * coeffs[0] * field
    for offset in range(1, 5):
        result = result + coeffs[offset] * (
            padded[:, 4 + offset : 4 + offset + tile_cols, 4 : 4 + tile_depth]
            + padded[:, 4 - offset : 4 - offset + tile_cols, 4 : 4 + tile_depth]
        )
        result = result + coeffs[offset] * (
            padded[:, 4 : 4 + tile_cols, 4 + offset : 4 + offset + tile_depth]
            + padded[:, 4 : 4 + tile_cols, 4 - offset : 4 - offset + tile_depth]
        )
    return result


def laplace_along(stress):
    tile_rows = stress.shape[0]
    padded = with_halo(stress, (("tile", 0),), 4)
    result = coeffs[0] * stress
    for offset in range(1, 5):
        result = result + coeffs[offset] * (
            padded[4 + offset : 4 + offset + tile_rows]
            + padded[4 - offset : 4 - offset + tile_rows]
        )
    return result


def shards(
    adjoint_now,
    adjoint_prev,
    costates,
    modulus,
    relaxation,
    absorb_mask,
    relax_rates,
    mech_weights,
    forward_lap,
    recv_cells,
    enc_signs,
    residuals,
):
    current = adjoint_now[0]
    previous = adjoint_prev[0]
    memory = costates[0]
    snaps = forward_lap[0]
    tile_rows, tile_cols, tile_depth = current.shape
    cell_count = tile_rows * tile_cols * tile_depth
    decay = jnp.exp(-relax_rates)[:, None, None, None]
    weights = mech_weights[:, None, None, None]
    damp = 1.0 - damping * absorb_mask.astype(jnp.float32)
    first_cell = lax.axis_index("tile") * cell_count
    local_cells = recv_cells[0] - first_cell
    in_range = (local_cells >= 0) & (local_cells < cell_count)
    targets = jnp.where(in_range, local_cells, cell_count)
    sources = jnp.sum(enc_signs[0].astype(jnp.float32)[:, None, None] * residuals[0], axis=0)
    grad_m = jnp.zeros((tile_rows, tile_cols, tile_depth), jnp.float32)
    grad_t = jnp.zeros((tile_rows, tile_cols, tile_depth), jnp.float32)
    for step_index in range(STEPS - 1, -1, -1):
        summed = jnp.sum(weights * memory, axis=0)
        stress = modulus * (current - relaxation * summed)
        lap = laplace_along(stress) + laplace_cross(stress)
        memory = decay * memory + (1.0 - decay) * current[None]
        inject = (
            jnp.zeros((cell_count,), jnp.float32)
            .at[targets]
            .add(sources[step_index], mode="drop")
            .reshape(tile_rows, tile_cols, tile_depth)
        )
        fresh = damp * (2.0 * current - previous + lap + inject)
        previous = current
        current = fresh
        snap = snaps[step_index].astype(jnp.float32)
        term_m = current * snap
        term_t = modulus * jnp.sum(weights * memory, axis=0) * snap
        grad_m = grad_m + term_m
        grad_t = grad_t + term_t
    owned_m, owned_t = (
        lax.psum_scatter(grad_m, "shot", scatter_dimension=1, tiled=True),
        lax.psum_scatter(grad_t, "shot", scatter_dimension=1, tiled=True),
    )
    return (current[None], owned_m, owned_t)


def solution(mesh):
    return jax.shard_map(
        shards,
        mesh=mesh,
        in_specs=(
            P("shot", "tile", None, None),
            P("shot", "tile", None, None),
            P("shot", None, "tile", None, None),
            P("tile", None, None),
            P("tile", None, None),
            P("tile", None, None),
            P(),
            P(),
            P("shot", None, "tile", None, None),
            P("shot", None),
            P("shot", None),
            P("shot", None, None, None),
        ),
        out_specs=(P("shot", "tile", None, None), P("tile", "shot", None), P("tile", "shot", None)),
        check_vma=False,
    )
```

profile of v0, /device:TPU:9, one launch (start us, length us, event | category | flops | bytes accessed | tf_op | source)
XLA Modules:
  0.0 148.3 jit_solution(6502466572556412979)
XLA Ops:
  7.2 0.0 reduce-scatter.5.cloned.1.call-start
  7.3 1.7 %fusion = f32[8,64,128]{2,1,0:T(8,128)S(1)} fusion(f32[1,6,8,64,128]{4,3,2,1,0:T(8,128)} %param.14, f32[6]{0:T(128)} %param.19), kind=kLoop, calls=%fused_computation.104 | loop fusion | flops 720896 | bytes 1835032 | tf_op jit(solution)/shard_map/reduce_sum | solution.py:85
  9.0 0.0 copy-start.3
  9.0 0.1 subtract_multiply_fusion.5
  9.1 0.7 fusion.309
  9.8 3.0 %collective-permute-start = (f32[4,64,128]{2,1,0:T(8,128)}, f32[4,64,128]{2,1,0:T(8,128)S(1)}, u32[]{:S(2)}, u32[]{:S(2)}) collective-permute-start(f32[4,64,128]{2,1,0:T(8,128)} %get-tuple-element.28), channel_id=1, source_target_pairs={{1,0},{2,1},{3,2},{4,3},{5,4},{6,5},{7,6},{9,8},{10,9},{11,10},{12... | collective-permute-start | bytes 393224 | tf_op jit(solution)/shard_map/ppermute | solution.py:21
  12.8 2.2 %collective-permute-start.1 = (f32[4,64,128]{2,1,0:T(8,128)S(1)}, f32[4,64,128]{2,1,0:T(8,128)S(1)}, u32[]{:S(2)}, u32[]{:S(2)}) collective-permute-start(f32[4,64,128]{2,1,0:T(8,128)S(1)} %get-tuple-element.29), channel_id=1, source_target_pairs={{0,1},{1,2},{2,3},{3,4},{4,5},{5,6},{6,7},{8,9},{9,10},{10,11},{11... | collective-permute-start | bytes 393224 | tf_op jit(solution)/shard_map/ppermute | solution.py:20
  15.1 0.1 fusion.300
  15.2 0.6 fusion.310
  15.8 0.6 compare_select_fusion
  16.4 3.5 %scatter_custom_fusion = f32[65536]{0:T(1024)S(1)} fusion(s32[512]{0:T(512)} %bitcast.84, f32[512]{0:T(512)S(1)} %bitcast.83, f32[]{:T(128)} %constant.16.clone.1), kind=kCustom, calls=%fused_computation.516 | custom fusion | flops 512 | bytes 262656 | tf_op jit(solution)/shard_map/scatter-add | solution.py:92
  19.9 0.7 negate_exponential_fusion
  20.6 0.6 copy-done.21
  21.2 1.8 %fusion.120 = f32[8,64,128]{2,1,0:T(8,128)S(1)} fusion(f32[8,64,128]{2,1,0:T(8,128)S(1)} %bitcast.72, f32[8,64,128]{2,1,0:T(8,128)S(1)} %subtract_multiply_fusion.5, f32[4,64,128]{2,1,0:T(8,128)} %copy-done.21, f32[4,64,128]{2,1,0:T(8,128)S(1)} %collective-permute-done, f32[1,8,64,128]{3,2,1,0:T(8,128)} %param.13, s32[8,64,128]{2,1,0:T(8,128)S(1)} %copy-done.3, ...), kind=kLoop, calls=%fused_computation.318 | loop fusion | flops 3604480 | bytes 1835008 | tf_op jit(solution)/shard_map/mul | solution.py:95
  23.0 0.6 multiply_reduce_fusion.4
  23.6 0.1 subtract_multiply_fusion.4
  23.7 0.8 copy-done.20
  24.5 0.7 fusion.308
  25.2 3.9 %collective-permute-start.2 = (f32[4,64,128]{2,1,0:T(8,128)}, f32[4,64,128]{2,1,0:T(8,128)S(1)}, u32[]{:S(2)}, u32[]{:S(2)}) collective-permute-start(f32[4,64,128]{2,1,0:T(8,128)} %get-tuple-element.26), channel_id=1, source_target_pairs={{1,0},{2,1},{3,2},{4,3},{5,4},{6,5},{7,6},{9,8},{10,9},{11,10},{12... | collective-permute-start | bytes 393224 | tf_op jit(solution)/shard_map/ppermute | solution.py:21
  29.1 2.0 %collective-permute-start.3 = (f32[4,64,128]{2,1,0:T(8,128)}, f32[4,64,128]{2,1,0:T(8,128)}, u32[]{:S(2)}, u32[]{:S(2)}) collective-permute-start(f32[4,64,128]{2,1,0:T(8,128)} %get-tuple-element.27), channel_id=1, source_target_pairs={{0,1},{1,2},{2,3},{3,4},{4,5},{5,6},{6,7},{8,9},{9,10},{10,11},{11... | collective-permute-start | bytes 393224 | tf_op jit(solution)/shard_map/ppermute | solution.py:20
  31.2 4.1 %scatter_custom_fusion.1 = f32[65536]{0:T(1024)} fusion(s32[512]{0:T(512)} %bitcast.85, f32[512]{0:T(512)} %bitcast.82, f32[]{:T(128)} %constant.16.clone.1), kind=kCustom, calls=%fused_computation.514 | custom fusion | flops 512 | bytes 262656 | tf_op jit(solution)/shard_map/scatter-add | solution.py:92
  35.2 1.0 collective-permute-done.3
  36.2 5.0 %subtract_multiply_fusion.3 = (f32[8,64,128]{2,1,0:T(8,128)S(1)}, f32[8,64,128]{2,1,0:T(8,128)S(1)}) fusion(f32[8,64,128]{2,1,0:T(8,128)S(1)} %copy-done.1, f32[8,64,128]{2,1,0:T(8,128)S(1)} %copy-done.2, f32[8,64,128]{2,1,0:T(8,128)S(1)} %get-tuple-element.5, f32[8,64,128]{2,1,0:T(8,128)} %bitcast.75, f32[8,64,128]{2,1,0:T(8,128)} %copy-done.20, ...), kind=kLoop, calls=%fused_computation.502 | loop fusion | flops 3801088 | bytes 2883584 | tf_op jit(solution)/shard_map/mul | solution.py:86
  41.2 0.7 copy-done.18
  41.9 0.7 fusion.307
  42.6 4.0 %collective-permute-start.4 = (f32[4,64,128]{2,1,0:T(8,128)}, f32[4,64,128]{2,1,0:T(8,128)S(1)}, u32[]{:S(2)}, u32[]{:S(2)}) collective-permute-start(f32[4,64,128]{2,1,0:T(8,128)} %get-tuple-element.24), channel_id=1, source_target_pairs={{1,0},{2,1},{3,2},{4,3},{5,4},{6,5},{7,6},{9,8},{10,9},{11,10},{12... | collective-permute-start | bytes 393224 | tf_op jit(solution)/shard_map/ppermute | solution.py:21
  46.5 2.0 %collective-permute-start.5 = (f32[4,64,128]{2,1,0:T(8,128)S(1)}, f32[4,64,128]{2,1,0:T(8,128)S(1)}, u32[]{:S(2)}, u32[]{:S(2)}) collective-permute-start(f32[4,64,128]{2,1,0:T(8,128)S(1)} %get-tuple-element.25), channel_id=1, source_target_pairs={{0,1},{1,2},{2,3},{3,4},{4,5},{5,6},{6,7},{8,9},{9,10},{10,11},{11... | collective-permute-start | bytes 393224 | tf_op jit(solution)/shard_map/ppermute | solution.py:20
  48.6 4.1 %scatter_custom_fusion.2 = f32[65536]{0:T(1024)} fusion(s32[512]{0:T(512)} %bitcast.86, f32[512]{0:T(512)} %bitcast.81, f32[]{:T(128)} %constant.16.clone.1), kind=kCustom, calls=%fused_computation.512 | custom fusion | flops 512 | bytes 262656 | tf_op jit(solution)/shard_map/scatter-add | solution.py:92
  52.7 0.6 collective-permute-done.5
  53.3 0.6 copy-done.22
  53.9 4.9 %fusion.80 = f32[8,64,128]{2,1,0:T(8,128)S(1)} fusion(f32[8,64,128]{2,1,0:T(8,128)} %bitcast.73, f32[8,64,128]{2,1,0:T(8,128)} %copy-done.18, f32[4,64,128]{2,1,0:T(8,128)} %copy-done.22, f32[4,64,128]{2,1,0:T(8,128)S(1)} %collective-permute-done.4, f32[8,64,128]{2,1,0:T(8,128)S(1)} %fusion.120, f32[8,64,128]{2,1,0:T(8,128)S(1)} %get-tuple-element.15, ...), kind=kLoop, calls=%fused_computation.278 | loop fusion | flops 3604480 | bytes 1835008 | tf_op jit(solution)/shard_map/mul | solution.py:95
  58.9 2.8 %multiply_reduce_fusion.2 = (f32[8,64,128]{2,1,0:T(8,128)}, f32[8,64,128]{2,1,0:T(8,128)S(1)}, f32[6,8,64,128]{3,2,1,0:T(8,128)}) fusion(f32[8,64,128]{2,1,0:T(8,128)S(1)} %fusion.80, f32[6]{0:T(128)S(1)} %get-tuple-element.37, f32[6]{0:T(128)S(1)} %get-tuple-element.36, f32[6]{0:T(128)S(1)} %copy-done.25, f32[8,64,128]{2,1,0:T(8,128)S(1)} %get-tuple-element.15, ...), kind=kLoop, calls=%fused_computation.109 | loop fusion | flops 6160384 | bytes 4718664 | tf_op jit(solution)/shard_map/reduce_sum | solution.py:85
  61.7 0.7 copy-done.10
  62.3 0.1 subtract_multiply_fusion.2
  62.4 4.5 %collective-permute-start.6 = (f32[4,64,128]{2,1,0:T(8,128)S(1)}, f32[4,64,128]{2,1,0:T(8,128)S(1)}, u32[]{:S(2)}, u32[]{:S(2)}) collective-permute-start(f32[4,64,128]{2,1,0:T(8,128)S(1)} %get-tuple-element.22), channel_id=1, source_target_pairs={{1,0},{2,1},{3,2},{4,3},{5,4},{6,5},{7,6},{9,8},{10,9},{11,10},{12... | collective-permute-start | bytes 393224 | tf_op jit(solution)/shard_map/ppermute | solution.py:21
  66.9 1.9 %collective-permute-start.7 = (f32[4,64,128]{2,1,0:T(8,128)S(1)}, f32[4,64,128]{2,1,0:T(8,128)S(1)}, u32[]{:S(2)}, u32[]{:S(2)}) collective-permute-start(f32[4,64,128]{2,1,0:T(8,128)S(1)} %get-tuple-element.23), channel_id=1, source_target_pairs={{0,1},{1,2},{2,3},{3,4},{4,5},{5,6},{6,7},{8,9},{9,10},{10,11},{11... | collective-permute-start | bytes 393224 | tf_op jit(solution)/shard_map/ppermute | solution.py:20
  68.9 3.5 %scatter_custom_fusion.3 = f32[65536]{0:T(1024)S(1)} fusion(s32[512]{0:T(512)} %bitcast.87, f32[512]{0:T(512)} %bitcast.80, f32[]{:T(128)} %constant.16.clone.1), kind=kCustom, calls=%fused_computation.510 | custom fusion | flops 512 | bytes 262656 | tf_op jit(solution)/shard_map/scatter-add | solution.py:92
  72.3 1.2 collective-permute-done.7
  73.5 1.4 subtract_multiply_fusion.1
  74.9 0.7 copy-done.19
  75.6 0.7 fusion.305
  76.3 4.4 %collective-permute-start.8 = (f32[4,64,128]{2,1,0:T(8,128)}, f32[4,64,128]{2,1,0:T(8,128)S(1)}, u32[]{:S(2)}, u32[]{:S(2)}) collective-permute-start(f32[4,64,128]{2,1,0:T(8,128)} %get-tuple-element.20), channel_id=1, source_target_pairs={{1,0},{2,1},{3,2},{4,3},{5,4},{6,5},{7,6},{9,8},{10,9},{11,10},{12... | collective-permute-start | bytes 393224 | tf_op jit(solution)/shard_map/ppermute | solution.py:21
  80.7 2.1 %collective-permute-start.9 = (f32[4,64,128]{2,1,0:T(8,128)S(1)}, f32[4,64,128]{2,1,0:T(8,128)S(1)}, u32[]{:S(2)}, u32[]{:S(2)}) collective-permute-start(f32[4,64,128]{2,1,0:T(8,128)S(1)} %get-tuple-element.21), channel_id=1, source_target_pairs={{0,1},{1,2},{2,3},{3,4},{4,5},{5,6},{6,7},{8,9},{9,10},{10,11},{11... | collective-permute-start | bytes 393224 | tf_op jit(solution)/shard_map/ppermute | solution.py:20
  82.8 4.1 %scatter_custom_fusion.4 = f32[65536]{0:T(1024)} fusion(s32[512]{0:T(512)} %bitcast.88, f32[512]{0:T(512)} %bitcast.79, f32[]{:T(128)} %constant.16.clone.1), kind=kCustom, calls=%fused_computation.508 | custom fusion | flops 512 | bytes 262656 | tf_op jit(solution)/shard_map/scatter-add | solution.py:92
  86.9 0.8 collective-permute-done.9
  87.8 0.6 copy-done.23
  88.4 6.7 %fusion.40 = f32[8,64,128]{2,1,0:T(8,128)S(1)} fusion(f32[8,64,128]{2,1,0:T(8,128)} %bitcast.74, f32[8,64,128]{2,1,0:T(8,128)} %copy-done.19, f32[4,64,128]{2,1,0:T(8,128)} %copy-done.23, f32[4,64,128]{2,1,0:T(8,128)S(1)} %collective-permute-done.8, f32[8,64,128]{2,1,0:T(8,128)S(1)} %fusion.80, f32[8,64,128]{2,1,0:T(8,128)} %get-tuple-element.12, ...), kind=kLoop, calls=%fused_computation.238 | loop fusion | flops 3604480 | bytes 1835008 | tf_op jit(solution)/shard_map/mul | solution.py:95
  95.1 0.7 multiply_reduce_fusion
  95.9 0.3 copy-done.8
  96.2 0.1 copy-done.11
  96.2 0.1 copy-done.13
  96.3 0.1 copy-done.15
  96.4 0.1 copy-done.17
  96.5 1.0 fusion.11
  97.5 0.0 reduce-scatter.5.cloned.1.call-update
  97.5 0.0 reduce-scatter.3.cloned.1.call-start
  97.6 4.2 %collective-permute-start.10 = (f32[4,64,128]{2,1,0:T(8,128)S(1)}, f32[4,64,128]{2,1,0:T(8,128)S(1)}, u32[]{:S(2)}, u32[]{:S(2)}) collective-permute-start(f32[4,64,128]{2,1,0:T(8,128)S(1)} %get-tuple-element.18), channel_id=1, source_target_pairs={{1,0},{2,1},{3,2},{4,3},{5,4},{6,5},{7,6},{9,8},{10,9},{11,10},{12... | collective-permute-start | bytes 393224 | tf_op jit(solution)/shard_map/ppermute | solution.py:21
  101.8 1.9 %collective-permute-start.11 = (f32[4,64,128]{2,1,0:T(8,128)S(1)}, f32[4,64,128]{2,1,0:T(8,128)S(1)}, u32[]{:S(2)}, u32[]{:S(2)}) collective-permute-start(f32[4,64,128]{2,1,0:T(8,128)S(1)} %get-tuple-element.19), channel_id=1, source_target_pairs={{0,1},{1,2},{2,3},{3,4},{4,5},{5,6},{6,7},{8,9},{9,10},{10,11},{11... | collective-permute-start | bytes 393224 | tf_op jit(solution)/shard_map/ppermute | solution.py:20
  103.7 3.5 %scatter_custom_fusion.5 = f32[65536]{0:T(1024)S(1)} fusion(s32[512]{0:T(512)} %bitcast.89, f32[512]{0:T(512)S(1)} %bitcast.78, f32[]{:T(128)} %constant.16.clone.1), kind=kCustom, calls=%fused_computation.506 | custom fusion | flops 512 | bytes 262656 | tf_op jit(solution)/shard_map/scatter-add | solution.py:92
  107.2 1.6 %collective-permute-done.11 = f32[4,64,128]{2,1,0:T(8,128)S(1)} collective-permute-done((f32[4,64,128]{2,1,0:T(8,128)S(1)}, f32[4,64,128]{2,1,0:T(8,128)S(1)}, u32[]{:S(2)}, u32[]{:S(2)}) %collective-permute-start.11) | collective-permute-done | bytes 131104 | tf_op jit(solution)/shard_map/ppermute | solution.py:20
  108.9 1.6 %fusion.6 = (f32[8,64,128]{2,1,0:T(8,128)}, f32[8,64,128]{2,1,0:T(8,128)}) fusion(f32[8,64,128]{2,1,0:T(8,128)S(1)} %fusion.120, f32[8,64,128]{2,1,0:T(8,128)S(1)} %get-tuple-element.15, f32[8,64,128]{2,1,0:T(8,128)S(1)} %fusion.80, f32[8,64,128]{2,1,0:T(8,128)S(1)} %copy-done.7, f32[8,64,128]{2,1,0:T(8,128)S(1)} %fusion.40, ...), kind=kLoop, calls=%fused_computation.204 | loop fusion | flops 4718592 | bytes 3670016 | tf_op jit(solution)/shard_map/add | solution.py:101
  110.4 0.0 reduce-scatter.3.cloned.1.call-update
  110.5 7.8 %reduce-scatter.5.cloned.1.call-done = f32[8,16,128]{2,1,0:T(8,128)} async-done(((f32[8,64,128]{2,1,0:T(8,128)}), f32[8,16,128]{2,1,0:T(8,128)}) %reduce-scatter.5.cloned.1.call-update) | async-done | bytes 65552 | tf_op jit(solution)/shard_map/reduce_scatter | solution.py:105
  118.2 23.2 %reduce-scatter.3.cloned.1.call-done = f32[8,16,128]{2,1,0:T(8,128)} async-done(((f32[8,64,128]{2,1,0:T(8,128)}), f32[8,16,128]{2,1,0:T(8,128)}) %reduce-scatter.3.cloned.1.call-update) | async-done | bytes 65552 | tf_op jit(solution)/shard_map/reduce_scatter | solution.py:104
  (53 shorter events, 0.2 us)
Async XLA Ops:
  7.2 1.8 %copy-start.4 = (f32[1,8,64,128]{3,2,1,0:T(8,128)S(1)}, f32[1,8,64,128]{3,2,1,0:T(8,128)}, u32[]{:S(2)}) copy-start(f32[1,8,64,128]{3,2,1,0:T(8,128)} %param.12) | copy-start | bytes 786436
  7.2 1.8 %copy-start.1 = (f32[8,64,128]{2,1,0:T(8,128)S(1)}, f32[8,64,128]{2,1,0:T(8,128)}, u32[]{:S(2)}) copy-start(f32[8,64,128]{2,1,0:T(8,128)} %param.15) | copy-start | bytes 786436
  7.2 1.8 %copy-start.2 = (f32[8,64,128]{2,1,0:T(8,128)S(1)}, f32[8,64,128]{2,1,0:T(8,128)}, u32[]{:S(2)}) copy-start(f32[8,64,128]{2,1,0:T(8,128)} %param.16) | copy-start | bytes 786436
  7.2 7.9 %copy-start.27 = (s32[1,8]{1,0:T(1,128)S(1)}, s32[1,8]{1,0:T(1,128)}, u32[]{:S(2)}) copy-start(s32[1,8]{1,0:T(1,128)} %param.22) | copy-start | bytes 100
  7.2 7.9 %copy-start.24 = (f32[1,8,6,512]{3,1,2,0:T(8,128)S(1)}, f32[1,8,6,512]{3,1,2,0:T(8,128)}, u32[]{:S(2)}) copy-start(f32[1,8,6,512]{3,1,2,0:T(8,128)} %param.23) | copy-start | bytes 294916
  7.2 8.6 %copy-start.26 = (s32[1,512]{1,0:T(1,128)S(1)}, s32[1,512]{1,0:T(1,128)}, u32[]{:S(2)}) copy-start(s32[1,512]{1,0:T(1,128)} %param.21) | copy-start | bytes 6148
  7.2 111.0 %reduce-scatter.5.cloned.1.call-start = ((), (), s32[]{:S(2)}) async-start(), calls=%async_computation.3 | async-start | bytes 327680 | tf_op jit(solution)/shard_map/reduce_scatter | solution.py:105
  9.0 12.2 %copy-start.3 = (s32[8,64,128]{2,1,0:T(8,128)S(1)}, s32[8,64,128]{2,1,0:T(8,128)}, u32[]{:S(2)}) copy-start(s32[8,64,128]{2,1,0:T(8,128)} %param.17) | copy-start | bytes 786436
  9.1 13.9 %copy-start = (f32[1,6,8,64,128]{4,3,2,1,0:T(8,128)S(1)}, f32[1,6,8,64,128]{4,3,2,1,0:T(8,128)}, u32[]{:S(2)}) copy-start(f32[1,6,8,64,128]{4,3,2,1,0:T(8,128)} %param.14) | copy-start | bytes 4718596
  9.1 13.9 %copy-start.25 = (f32[6]{0:T(128)S(1)}, f32[6]{0:T(128)}, u32[]{:S(2)}) copy-start(f32[6]{0:T(128)} %param.19) | copy-start | bytes 76
  9.8 10.8 %collective-permute-start = (f32[4,64,128]{2,1,0:T(8,128)}, f32[4,64,128]{2,1,0:T(8,128)S(1)}, u32[]{:S(2)}, u32[]{:S(2)}) collective-permute-start(f32[4,64,128]{2,1,0:T(8,128)} %get-tuple-element.28), channel_id=1, source_target_pairs={{1,0},{2,1},{3,2},{4,3},{5,4},{6,5},{7,6},{9,8},{10,9},{11,10},{12... | collective-permute-start | bytes 393224 | tf_op jit(solution)/shard_map/ppermute | solution.py:21
  12.8 7.7 %collective-permute-start.1 = (f32[4,64,128]{2,1,0:T(8,128)S(1)}, f32[4,64,128]{2,1,0:T(8,128)S(1)}, u32[]{:S(2)}, u32[]{:S(2)}) collective-permute-start(f32[4,64,128]{2,1,0:T(8,128)S(1)} %get-tuple-element.29), channel_id=1, source_target_pairs={{0,1},{1,2},{2,3},{3,4},{4,5},{5,6},{6,7},{8,9},{9,10},{10,11},{11... | collective-permute-start | bytes 393224 | tf_op jit(solution)/shard_map/ppermute | solution.py:20
  20.6 0.7 copy-start.21
  23.6 12.6 %copy-start.12 = (f32[8,64,128]{2,1,0:T(8,128)}, f32[8,64,128]{2,1,0:T(8,128)S(1)}, u32[]{:S(2)}) copy-start(f32[8,64,128]{2,1,0:T(8,128)S(1)} %get-tuple-element.6) | copy-start | bytes 786436
  23.6 17.6 %copy-start.16 = (f32[8,64,128]{2,1,0:T(8,128)}, f32[8,64,128]{2,1,0:T(8,128)S(1)}, u32[]{:S(2)}) copy-start(f32[8,64,128]{2,1,0:T(8,128)S(1)} %get-tuple-element.5) | copy-start | bytes 786436
  23.7 0.8 copy-start.20
  25.2 10.1 %collective-permute-start.2 = (f32[4,64,128]{2,1,0:T(8,128)}, f32[4,64,128]{2,1,0:T(8,128)S(1)}, u32[]{:S(2)}, u32[]{:S(2)}) collective-permute-start(f32[4,64,128]{2,1,0:T(8,128)} %get-tuple-element.26), channel_id=1, source_target_pairs={{1,0},{2,1},{3,2},{4,3},{5,4},{6,5},{7,6},{9,8},{10,9},{11,10},{12... | collective-permute-start | bytes 393224 | tf_op jit(solution)/shard_map/ppermute | solution.py:21
  29.1 7.1 %collective-permute-start.3 = (f32[4,64,128]{2,1,0:T(8,128)}, f32[4,64,128]{2,1,0:T(8,128)}, u32[]{:S(2)}, u32[]{:S(2)}) collective-permute-start(f32[4,64,128]{2,1,0:T(8,128)} %get-tuple-element.27), channel_id=1, source_target_pairs={{0,1},{1,2},{2,3},{3,4},{4,5},{5,6},{6,7},{8,9},{9,10},{10,11},{11... | collective-permute-start | bytes 393224 | tf_op jit(solution)/shard_map/ppermute | solution.py:20
  41.2 0.7 copy-start.18
  42.6 10.1 %collective-permute-start.4 = (f32[4,64,128]{2,1,0:T(8,128)}, f32[4,64,128]{2,1,0:T(8,128)S(1)}, u32[]{:S(2)}, u32[]{:S(2)}) collective-permute-start(f32[4,64,128]{2,1,0:T(8,128)} %get-tuple-element.24), channel_id=1, source_target_pairs={{1,0},{2,1},{3,2},{4,3},{5,4},{6,5},{7,6},{9,8},{10,9},{11,10},{12... | collective-permute-start | bytes 393224 | tf_op jit(solution)/shard_map/ppermute | solution.py:21
  46.5 6.7 %collective-permute-start.5 = (f32[4,64,128]{2,1,0:T(8,128)S(1)}, f32[4,64,128]{2,1,0:T(8,128)S(1)}, u32[]{:S(2)}, u32[]{:S(2)}) collective-permute-start(f32[4,64,128]{2,1,0:T(8,128)S(1)} %get-tuple-element.25), channel_id=1, source_target_pairs={{0,1},{1,2},{2,3},{3,4},{4,5},{5,6},{6,7},{8,9},{9,10},{10,11},{11... | collective-permute-start | bytes 393224 | tf_op jit(solution)/shard_map/ppermute | solution.py:20
  53.3 0.6 copy-start.22
  61.7 0.7 copy-start.10
  61.7 11.9 %copy-start.14 = (f32[8,64,128]{2,1,0:T(8,128)S(1)}, f32[8,64,128]{2,1,0:T(8,128)}, u32[]{:S(2)}) copy-start(f32[8,64,128]{2,1,0:T(8,128)} %get-tuple-element.7) | copy-start | bytes 786436
  62.4 9.9 %collective-permute-start.6 = (f32[4,64,128]{2,1,0:T(8,128)S(1)}, f32[4,64,128]{2,1,0:T(8,128)S(1)}, u32[]{:S(2)}, u32[]{:S(2)}) collective-permute-start(f32[4,64,128]{2,1,0:T(8,128)S(1)} %get-tuple-element.22), channel_id=1, source_target_pairs={{1,0},{2,1},{3,2},{4,3},{5,4},{6,5},{7,6},{9,8},{10,9},{11,10},{12... | collective-permute-start | bytes 393224 | tf_op jit(solution)/shard_map/ppermute | solution.py:21
  66.9 6.6 %collective-permute-start.7 = (f32[4,64,128]{2,1,0:T(8,128)S(1)}, f32[4,64,128]{2,1,0:T(8,128)S(1)}, u32[]{:S(2)}, u32[]{:S(2)}) collective-permute-start(f32[4,64,128]{2,1,0:T(8,128)S(1)} %get-tuple-element.23), channel_id=1, source_target_pairs={{0,1},{1,2},{2,3},{3,4},{4,5},{5,6},{6,7},{8,9},{9,10},{10,11},{11... | collective-permute-start | bytes 393224 | tf_op jit(solution)/shard_map/ppermute | solution.py:20
  74.9 0.7 copy-start.19
  74.9 20.2 %copy-start.5 = (f32[6,8,64,128]{3,2,1,0:T(8,128)S(1)}, f32[6,8,64,128]{3,2,1,0:T(8,128)}, u32[]{:S(2)}) copy-start(f32[6,8,64,128]{3,2,1,0:T(8,128)} %get-tuple-element.13) | copy-start | bytes 4718596
  76.3 10.6 %collective-permute-start.8 = (f32[4,64,128]{2,1,0:T(8,128)}, f32[4,64,128]{2,1,0:T(8,128)S(1)}, u32[]{:S(2)}, u32[]{:S(2)}) collective-permute-start(f32[4,64,128]{2,1,0:T(8,128)} %get-tuple-element.20), channel_id=1, source_target_pairs={{1,0},{2,1},{3,2},{4,3},{5,4},{6,5},{7,6},{9,8},{10,9},{11,10},{12... | collective-permute-start | bytes 393224 | tf_op jit(solution)/shard_map/ppermute | solution.py:21
  80.7 7.0 %collective-permute-start.9 = (f32[4,64,128]{2,1,0:T(8,128)S(1)}, f32[4,64,128]{2,1,0:T(8,128)S(1)}, u32[]{:S(2)}, u32[]{:S(2)}) collective-permute-start(f32[4,64,128]{2,1,0:T(8,128)S(1)} %get-tuple-element.21), channel_id=1, source_target_pairs={{0,1},{1,2},{2,3},{3,4},{4,5},{5,6},{6,7},{8,9},{9,10},{10,11},{11... | collective-permute-start | bytes 393224 | tf_op jit(solution)/shard_map/ppermute | solution.py:20
  86.9 8.2 %copy-start.6 = (f32[8,64,128]{2,1,0:T(8,128)S(1)}, f32[8,64,128]{2,1,0:T(8,128)}, u32[]{:S(2)}) copy-start(f32[8,64,128]{2,1,0:T(8,128)} %get-tuple-element.12) | copy-start | bytes 786436
  87.7 0.6 copy-start.23
  95.1 1.1 copy-start.8
  95.1 1.2 copy-start.11
  95.1 1.2 copy-start.13
  95.1 1.3 copy-start.15
  95.1 1.4 copy-start.17
  96.5 12.4 %copy-start.7 = (f32[8,64,128]{2,1,0:T(8,128)S(1)}, f32[8,64,128]{2,1,0:T(8,128)}, u32[]{:S(2)}) copy-start(f32[8,64,128]{2,1,0:T(8,128)} %get-tuple-element.12) | copy-start | bytes 786436
  96.5 12.4 %copy-start.9 = (bf16[1,6,8,64,128]{4,3,2,1,0:T(8,128)(2,1)S(1)}, bf16[1,6,8,64,128]{4,3,2,1,0:T(8,128)(2,1)}, u32[]{:S(2)}) copy-start(bf16[1,6,8,64,128]{4,3,2,1,0:T(8,128)(2,1)} %param.20) | copy-start | bytes 2359300
  97.5 43.9 %reduce-scatter.3.cloned.1.call-start = ((), (), s32[]{:S(2)}) async-start(), calls=%async_computation.2 | async-start | bytes 327680 | tf_op jit(solution)/shard_map/reduce_scatter | solution.py:104
  97.6 9.6 %collective-permute-start.10 = (f32[4,64,128]{2,1,0:T(8,128)S(1)}, f32[4,64,128]{2,1,0:T(8,128)S(1)}, u32[]{:S(2)}, u32[]{:S(2)}) collective-permute-start(f32[4,64,128]{2,1,0:T(8,128)S(1)} %get-tuple-element.18), channel_id=1, source_target_pairs={{1,0},{2,1},{3,2},{4,3},{5,4},{6,5},{7,6},{9,8},{10,9},{11,10},{12... | collective-permute-start | bytes 393224 | tf_op jit(solution)/shard_map/ppermute | solution.py:21
  101.8 7.1 %collective-permute-start.11 = (f32[4,64,128]{2,1,0:T(8,128)S(1)}, f32[4,64,128]{2,1,0:T(8,128)S(1)}, u32[]{:S(2)}, u32[]{:S(2)}) collective-permute-start(f32[4,64,128]{2,1,0:T(8,128)S(1)} %get-tuple-element.19), channel_id=1, source_target_pairs={{0,1},{1,2},{2,3},{3,4},{4,5},{5,6},{6,7},{8,9},{9,10},{10,11},{11... | collective-permute-start | bytes 393224 | tf_op jit(solution)/shard_map/ppermute | solution.py:20
Sparse Core Ops, SparseCore 0:
  97.7 20.5 reduce-scatter.4
  121.4 20.0 reduce-scatter.2
where the time goes:
time: 151 us; the launch traced here: 148 us
  other arithmetic  52.3 us (35%)
  starting transfers between devices  36.3 us (24%)
  waiting for transfers between devices  36.3 us (24%)
  between operations  14.5 us (10%)
  local copies, waits for them, and re-layouts  8.86 us (6%)
    ppermute x6, starting transfers between devices, with_halo(): after = lax.ppermute(leading, axis, down)  24 us
    reduce_scatter x1, waiting for transfers between devices, shards(): lax.psum_scatter(grad_m, 'shot', scatter_dimension=1, tiled=True)  23.2 us
    scatter-add x6, other arithmetic, shards(): inject = jnp.zeros((cell_count,), jnp.float32).at[targets].add(sources[st...  22.6 us
    mul x3, other arithmetic, shards(): fresh = damp * (2.0 * current - previous + lap + inject)  13.4 us
    ppermute x6, starting transfers between devices, with_halo(): before = lax.ppermute(last, axis, up)  12.3 us
    reduce_scatter x1, waiting for transfers between devices, shards(): lax.psum_scatter(grad_t, 'shot', scatter_dimension=1, tiled=True)  7.77 us
    mul x5, other arithmetic, shards(): stress = modulus * (current - relaxation * summed)  6.55 us
    unnamed x56, local copies, waits for them, and re-layouts  5.5 us
  transfers between devices with their start and end apart: 14, of which 7 were waited for; matrix products, arithmetic and copies ran while one was open for 18% of the time, Pallas kernels for 0%

commit v1 on v0

v1 whole, which is shorter than its diff:
```python
import functools

import jax
import jax.numpy as jnp
from jax import lax
from jax.experimental import pallas as pl
from jax.experimental.pallas import tpu as pltpu
from jax.sharding import PartitionSpec as P

MESH = pl.DeviceIdType.MESH
coeffs = (-205.0 / 72.0, 8.0 / 5.0, -1.0 / 5.0, 8.0 / 315.0, -1.0 / 560.0)
damping = 0.2
CHUNKS = 4
PAD = 8


def kernel(
    shots,
    tiles,
    now_ref,
    prev_ref,
    cost_ref,
    mod_ref,
    relax_ref,
    mask_ref,
    rates_ref,
    weights_ref,
    snaps_ref,
    cells_ref,
    signs_ref,
    resid_ref,
    out_ref,
    own_m_ref,
    own_t_ref,
    stress,
    halo,
    memory,
    adj,
    prev,
    damp,
    base,
    relaxed,
    grad_m,
    grad_t,
    send_m,
    send_t,
    got_m,
    got_t,
    parts,
    low_hot,
    vecs,
    halo_send,
    halo_recv,
    m_send,
    m_recv,
    t_send,
    t_recv,
):
    steps = snaps_ref.shape[1]
    mechs = cost_ref.shape[1]
    rows, cols, depth = mod_ref.shape
    half = rows // 2
    wide = cols // CHUNKS
    per = shots // CHUNKS
    owned = cols // shots
    receivers = cells_ref.shape[1]
    me = lax.axis_index("shot")
    tile = lax.axis_index("tile")
    has = (tile > 0, tile < tiles - 1)
    partner = (tile - 1, tile + 1)

    barrier = pltpu.get_barrier_semaphore()
    for side in range(2):

        @pl.when(has[side])
        def _(side=side):
            pl.semaphore_signal(barrier, inc=1, device_id={"tile": partner[side]}, device_id_type=MESH)

    for away in range(1, shots):
        pl.semaphore_signal(
            barrier, inc=1, device_id={"shot": lax.rem(me + away, shots)}, device_id_type=MESH
        )

    def halo_copy(k, side, start):
        return pltpu.make_async_remote_copy(
            src_ref=stress.at[k, pl.ds(side * half, half), pl.ds(pl.multiple_of(start + PAD, 8), wide), :],
            dst_ref=halo.at[k, 1 - side, :, pl.ds(start, wide), :],
            send_sem=halo_send.at[k, side, start // wide],
            recv_sem=halo_recv.at[k, 1 - side, start // wide],
            device_id={"tile": partner[side]},
            device_id_type=MESH,
        )

    def send_halo(k, side, start):
        @pl.when(has[side])
        def _():
            halo_copy(k, side, start).start()

    def wait_halo(k, side, start):
        @pl.when(has[side])
        def _():
            pltpu.make_async_remote_copy(
                src_ref=stress.at[k, pl.ds(side * half, half), pl.ds(pl.multiple_of(start + PAD, 8), wide), :],
                dst_ref=halo.at[k, side, :, pl.ds(start, wide), :],
                send_sem=halo_send.at[k, side, start // wide],
                recv_sem=halo_recv.at[k, side, start // wide],
                device_id={"tile": partner[side]},
                device_id_type=MESH,
            ).wait_recv()

    def m_copy(owner, source, side):
        return pltpu.make_async_remote_copy(
            src_ref=send_m.at[owner, pl.ds(side * half, half)],
            dst_ref=got_m.at[source, pl.ds(side * half, half)],
            send_sem=m_send.at[owner, side],
            recv_sem=m_recv.at[source, side],
            device_id={"shot": owner},
            device_id_type=MESH,
        )

    def t_copy(owner, source):
        return pltpu.make_async_remote_copy(
            src_ref=send_t.at[owner],
            dst_ref=got_t.at[source],
            send_sem=t_send.at[owner],
            recv_sem=t_recv.at[source],
            device_id={"shot": owner},
            device_id_type=MESH,
        )

    first = lax.rem(me // per + 1, CHUNKS)

    def chunk_of(c):
        return lax.rem(first + c, CHUNKS)

    for m in range(mechs):
        decay = jnp.exp(jnp.full((1, depth), -rates_ref[m], jnp.float32))
        weight = jnp.full((1, depth), weights_ref[m], jnp.float32)
        vecs[m] = decay
        vecs[mechs + m] = weight * (1.0 - decay)
        vecs[2 * mechs + m] = weight
    lane = lax.broadcasted_iota(jnp.int32, (1, depth), 1)
    for k in range(1, 5):
        vecs[3 * mechs + k - 1] = jnp.where(lane >= k, coeffs[k], 0.0)
        vecs[3 * mechs + 3 + k] = jnp.where(lane < depth - k, coeffs[k], 0.0)

    def begin(c, carry):
        chunk = chunk_of(c)
        start = pl.multiple_of(chunk * wide, wide)
        at = pl.ds(start, wide)
        padded = pl.ds(pl.multiple_of(start + PAD, 8), wide)
        total = None
        for m in range(mechs):
            value = vecs[2 * mechs + m] * cost_ref[0, m, :, at, :]
            memory[m, :, at, :] = value
            total = value if total is None else total + value
        now = now_ref[0, :, at, :]
        adj[:, at, :] = now
        stress[0, :, padded, :] = mod_ref[:, at, :] * (now - relax_ref[:, at, :] * total)
        return carry

    lax.fori_loop(0, CHUNKS, begin, 0)

    peers = shots - 1 + has[0].astype(jnp.int32) + has[1].astype(jnp.int32)
    pl.semaphore_wait(barrier, peers)

    def begin_send(c, carry):
        start = pl.multiple_of(chunk_of(c) * wide, wide)
        for side in range(2):
            send_halo(0, side, start)
        return carry

    lax.fori_loop(0, CHUNKS, begin_send, 0)

    empty = jnp.zeros((rows, PAD, depth), jnp.float32)

    def clear(k, carry):
        stress[k, :, 0:PAD, :] = empty
        stress[k, :, PAD + cols :, :] = empty
        for side in range(2):

            @pl.when(jnp.logical_not(has[side]))
            def _(side=side):
                halo[k, side] = jnp.zeros((half, cols, depth), jnp.float32)

        return carry

    lax.fori_loop(0, steps, clear, 0)

    sources = None
    for e in range(signs_ref.shape[1]):
        term = signs_ref[0, e].astype(jnp.float32) * resid_ref[0, e]
        sources = term if sources is None else sources + term
    for p in range(3):
        piece = sources.astype(jnp.bfloat16).astype(jnp.float32)
        for k in range(steps):
            parts[k, p : p + 1, :] = piece[steps - 1 - k : steps - k]
        sources = sources - piece
    cell = cells_ref[...] - tile * (rows * cols * depth)
    high = cell >> 7
    low = cell & 127
    low_hot[...] = jnp.where(
        lax.broadcasted_iota(jnp.int32, (depth, receivers), 0) == low, 1.0, 0.0
    ).astype(jnp.bfloat16)

    def prepare(c, carry):
        at = pl.ds(pl.multiple_of(c * wide, wide), wide)
        damp[:, at, :] = 1.0 - damping * mask_ref[:, at, :].astype(jnp.float32)
        prev[:, at, :] = prev_ref[0, :, at, :]
        grad_m[:, at, :] = jnp.zeros((rows, wide, depth), jnp.float32)
        grad_t[:, at, :] = jnp.zeros((rows, wide, depth), jnp.float32)
        return carry

    lax.fori_loop(0, CHUNKS, prepare, 0)

    def before(k, c, last):
        chunk = chunk_of(c)
        start = pl.multiple_of(chunk * wide, wide)
        at = pl.ds(start, wide)
        index = lax.broadcasted_iota(jnp.int32, (rows * wide, receivers), 0)
        spot = (index // wide) * cols + lax.rem(index, wide) + start
        hot = spot == high
        inject = None
        for p in range(3):
            left = jnp.where(hot, parts[k, p : p + 1, :], 0.0).astype(jnp.bfloat16)
            term = lax.dot_general(
                left, low_hot[...], (((1,), (1,)), ((), ())), preferred_element_type=jnp.float32
            )
            inject = term if inject is None else inject + term
        inject = inject.reshape(rows, wide, depth)
        window = stress[k, :, pl.ds(start, wide + 2 * PAD), :]
        center = window[:, PAD : PAD + wide]
        zeros = jnp.zeros((4, wide, depth), jnp.float32)
        tall = jnp.concatenate([zeros, center, zeros], axis=0)
        lap = (3.0 * coeffs[0]) * center
        for j in range(1, 5):
            near = window[:, PAD + j : PAD + j + wide] + window[:, PAD - j : PAD - j + wide]
            near = near + (tall[4 + j : 4 + j + rows] + tall[4 - j : 4 - j + rows])
            lap = lap + coeffs[j] * near
            lap = lap + vecs[3 * mechs + j - 1] * pltpu.roll(center, j, 2)
            lap = lap + vecs[3 * mechs + 3 + j] * pltpu.roll(center, depth - j, 2)
        now = adj[:, at, :]
        base[:, at, :] = damp[:, at, :] * (2.0 * now - prev[:, at, :] + lap + inject)
        prev[:, at, :] = now
        total = None
        for m in range(mechs):
            value = vecs[m] * memory[m, :, at, :] + vecs[mechs + m] * now
            memory[m, :, at, :] = value
            total = value if total is None else total + value
        weighted = mod_ref[:, at, :] * total
        relaxed[:, at, :] = relax_ref[:, at, :] * weighted
        gained = grad_t[:, at, :] + weighted * snaps_ref[0, steps - 1 - k, :, at, :].astype(jnp.float32)
        if last:
            for i in range(per):
                owner = chunk * per + i
                send_t[owner] = gained[:, i * owned : (i + 1) * owned, :]

                @pl.when(owner != me)
                def _(owner=owner):
                    t_copy(owner, me).start()
        else:
            grad_t[:, at, :] = gained

    def after(k, c, last):
        chunk = chunk_of(c)
        start = pl.multiple_of(chunk * wide, wide)
        at = pl.ds(start, wide)
        for side in range(2):
            wait_halo(k, side, start)
            lines = pl.ds(side * half, half)
            near = halo[k, side, :, at, :]
            zeros = jnp.zeros((4, wide, depth), jnp.float32)
            extra = None
            for j in range(1, 5):
                if side == 0:
                    shifted = jnp.concatenate([near, zeros], axis=0)[4 - j : 8 - j]
                else:
                    shifted = jnp.concatenate([zeros, near], axis=0)[j : 4 + j]
                term = coeffs[j] * shifted
                extra = term if extra is None else extra + term
            fresh = base[lines, at, :] + damp[lines, at, :] * extra
            gained = grad_m[lines, at, :] + fresh * snaps_ref[0, steps - 1 - k, lines, at, :].astype(jnp.float32)
            if last:
                out_ref[0, lines, at, :] = fresh
                for i in range(per):
                    owner = chunk * per + i
                    send_m[owner, lines] = gained[:, i * owned : (i + 1) * owned, :]

                    @pl.when(owner != me)
                    def _(owner=owner, side=side):
                        m_copy(owner, me, side).start()
            else:
                padded = pl.ds(pl.multiple_of(start + PAD, 8), wide)
                stress[k + 1, lines, padded, :] = mod_ref[lines, at, :] * fresh - relaxed[lines, at, :]
                send_halo(k + 1, side, start)
                adj[lines, at, :] = fresh
                grad_m[lines, at, :] = gained

    def loop(k, body, last):
        def one(c, carry):
            body(k, c, last)
            return carry

        lax.fori_loop(0, CHUNKS, one, 0)

    def step(k, carry):
        loop(k, before, False)
        loop(k, after, False)
        return carry

    lax.fori_loop(0, steps - 1, step, 0)
    loop(steps - 1, before, True)
    loop(steps - 1, after, True)

    total_t = send_t[me]
    for away in range(1, shots):
        source = lax.rem(me + away, shots)
        t_copy(source, source).wait_recv()
        total_t = total_t + got_t[source]
    own_t_ref[...] = total_t
    total_m = send_m[me]
    for away in range(1, shots):
        source = lax.rem(me + away, shots)
        for side in range(2):
            m_copy(source, source, side).wait_recv()
        total_m = total_m + got_m[source]
    own_m_ref[...] = total_m

    def finish(k, carry):
        for side in range(2):
            for c in range(CHUNKS):

                @pl.when(has[side])
                def _():
                    halo_copy(k, side, c * wide).wait_send()

        return carry

    lax.fori_loop(0, steps, finish, 0)
    for away in range(1, shots):
        owner = lax.rem(me + away, shots)
        t_copy(owner, me).wait_send()
        for side in range(2):
            m_copy(owner, me, side).wait_send()


def solution(mesh):
    shots = mesh.shape["shot"]
    tiles = mesh.shape["tile"]

    def shards(*args):
        now, _, costates, modulus, _, _, _, _, snaps, cells, _, _ = args
        rows, cols, depth = modulus.shape
        mechs = costates.shape[1]
        steps = snaps.shape[1]
        receivers = cells.shape[1]
        owned = cols // shots
        field = pltpu.VMEM((rows, cols, depth), jnp.float32)
        blocks = pltpu.VMEM((shots, rows, owned, depth), jnp.float32)
        vmem = pl.BlockSpec(memory_space=pltpu.VMEM)
        smem = pl.BlockSpec(memory_space=pltpu.SMEM)
        return pl.pallas_call(
            functools.partial(kernel, shots, tiles),
            out_shape=(
                jax.ShapeDtypeStruct(now.shape, jnp.float32),
                jax.ShapeDtypeStruct((rows, owned, depth), jnp.float32),
                jax.ShapeDtypeStruct((rows, owned, depth), jnp.float32),
            ),
            in_specs=[vmem] * 6 + [smem] * 2 + [vmem] * 2 + [smem, vmem],
            out_specs=(vmem, vmem, vmem),
            scratch_shapes=[
                pltpu.VMEM((steps, rows, cols + 2 * PAD, depth), jnp.float32),
                pltpu.VMEM((steps, 2, rows // 2, cols, depth), jnp.float32),
                pltpu.VMEM((mechs, rows, cols, depth), jnp.float32),
                field,
                field,
                field,
                field,
                field,
                field,
                field,
                blocks,
                blocks,
                blocks,
                blocks,
                pltpu.VMEM((steps, 8, receivers), jnp.float32),
                pltpu.VMEM((depth, receivers), jnp.bfloat16),
                pltpu.VMEM((3 * mechs + 8, 1, depth), jnp.float32),
                pltpu.SemaphoreType.DMA((steps, 2, CHUNKS)),
                pltpu.SemaphoreType.DMA((steps, 2, CHUNKS)),
                pltpu.SemaphoreType.DMA((shots, 2)),
                pltpu.SemaphoreType.DMA((shots, 2)),
                pltpu.SemaphoreType.DMA((shots,)),
                pltpu.SemaphoreType.DMA((shots,)),
            ],
            compiler_params=pltpu.CompilerParams(
                collective_id=0, has_side_effects=True, vmem_limit_bytes=40 * 1024 * 1024
            ),
        )(*args)

    return jax.shard_map(
        shards,
        mesh=mesh,
        in_specs=(
            P("shot", "tile", None, None),
            P("shot", "tile", None, None),
            P("shot", None, "tile", None, None),
            P("tile", None, None),
            P("tile", None, None),
            P("tile", None, None),
            P(),
            P(),
            P("shot", None, "tile", None, None),
            P("shot", None),
            P("shot", None),
            P("shot", None, None, None),
        ),
        out_specs=(P("shot", "tile", None, None), P("tile", "shot", None), P("tile", "shot", None)),
        check_vma=False,
    )
```

time: 151 us -> 57.5 us (0.38); the launches traced: 148 us -> 57.1 us
  other arithmetic: 52.3 us -> 0 us
  Pallas kernels: 0 us -> 43.6 us
  starting transfers between devices: 36.3 us -> 0 us
  waiting for transfers between devices: 36.3 us -> 0 us
  between operations: 14.5 us -> 0.66 us
  local copies, waits for them, and re-layouts: 8.86 us -> 12.8 us
    pallas_call x0 -> x1, Pallas kernels: none -> 43.6 us  [shards(): pl.pallas_call(functools.partial(kernel, shots, tiles), out_shape=(jax.Sh...]
    ppermute x12 -> x0, starting transfers between devices: 36.2 us -> none  [the longest x6 24 us: with_halo(): after = lax.ppermute(leading, axis, down)]
    reduce_scatter x2 -> x0, waiting for transfers between devices: 31 us -> none  [the longest x1 23.2 us: shards(): lax.psum_scatter(grad_m, 'shot', scatter_dimension=1, tiled=True)]
    scatter-add x6 -> x0, other arithmetic: 22.6 us -> none  [shards(): inject = jnp.zeros((cell_count,), jnp.float32).at[targets].add(sources[st...]
    mul x8 -> x0, other arithmetic: 19.9 us -> none  [the longest x3 13.4 us: shards(): fresh = damp * (2.0 * current - previous + lap + inject)]
    unnamed x56 -> x26, local copies, waits for them, and re-layouts: 5.5 us -> 12.8 us
    reduce_sum x5 -> x0, other arithmetic: 5.9 us -> none  [the longest x3 5.06 us: shards(): summed = jnp.sum(weights * memory, axis=0)]
    ppermute x12 -> x0, waiting for transfers between devices: 5.27 us -> none  [the longest x6 5.25 us: with_halo(): before = lax.ppermute(last, axis, up)]
  transfers between devices with their start and end apart: 14 -> 0, of which waited for: 7 -> 0; matrix products, arithmetic and copies ran while one was open for 18% -> 0% of each run, Pallas kernels for 0% -> 0%
where the time goes in v1:
time: 57.5 us; the launch traced here: 57.1 us
  Pallas kernels  43.6 us (76%)
  local copies, waits for them, and re-layouts  12.8 us (22%)
  between operations  0.66 us (1%)
    pallas_call x1, Pallas kernels, shards(): pl.pallas_call(functools.partial(kernel, shots, tiles), out_shape=(jax.Sh...  43.6 us
    unnamed x26, local copies, waits for them, and re-layouts  12.8 us

profile of v1, /device:TPU:9, one launch (start us, length us, event | category | flops | bytes accessed | tf_op | source)
XLA Modules:
  0.0 57.1 jit_solution(1045140458543658143)
XLA Ops:
  0.6 1.0 %copy.15.resid_ref = f32[1,8,6,512]{3,2,1,0:T(8,128)S(1)} copy(f32[1,8,6,512]{3,1,2,0:T(8,128)} %param.23) | data formatting | bytes 196608 | tf_op args[11]
  1.6 0.0 copy-start
  1.6 1.4 %copy-done = f32[1,6,8,64,128]{4,3,2,1,0:T(8,128)S(1)} copy-done((f32[1,6,8,64,128]{4,3,2,1,0:T(8,128)S(1)}, f32[1,6,8,64,128]{4,3,2,1,0:T(8,128)}, u32[]{:S(2)}) %copy-start) | copy-done | bytes 1572888
  3.0 0.0 copy-start.1
  3.0 1.1 %copy-done.1 = bf16[1,6,8,64,128]{4,3,2,1,0:T(8,128)(2,1)S(1)} copy-done((bf16[1,6,8,64,128]{4,3,2,1,0:T(8,128)(2,1)S(1)}, bf16[1,6,8,64,128]{4,3,2,1,0:T(8,128)(2,1)}, u32[]{:S(2)}) %copy-start.1) | copy-done | bytes 786456
  4.1 0.0 copy-start.2
  4.1 0.9 %copy-done.2 = f32[1,8,64,128]{3,2,1,0:T(8,128)S(1)} copy-done((f32[1,8,64,128]{3,2,1,0:T(8,128)S(1)}, f32[1,8,64,128]{3,2,1,0:T(8,128)}, u32[]{:S(2)}) %copy-start.2) | copy-done | bytes 262168
  5.1 0.0 copy-start.3
  5.1 0.9 %copy-done.3 = f32[1,8,64,128]{3,2,1,0:T(8,128)S(1)} copy-done((f32[1,8,64,128]{3,2,1,0:T(8,128)S(1)}, f32[1,8,64,128]{3,2,1,0:T(8,128)}, u32[]{:S(2)}) %copy-start.3) | copy-done | bytes 262168
  6.0 0.0 copy-start.4
  6.0 0.9 %copy-done.4 = f32[8,64,128]{2,1,0:T(8,128)S(1)} copy-done((f32[8,64,128]{2,1,0:T(8,128)S(1)}, f32[8,64,128]{2,1,0:T(8,128)}, u32[]{:S(2)}) %copy-start.4) | copy-done | bytes 262168
  7.0 0.0 copy-start.5
  7.0 0.9 %copy-done.5 = f32[8,64,128]{2,1,0:T(8,128)S(1)} copy-done((f32[8,64,128]{2,1,0:T(8,128)S(1)}, f32[8,64,128]{2,1,0:T(8,128)}, u32[]{:S(2)}) %copy-start.5) | copy-done | bytes 262168
  7.9 0.0 copy-start.6
  7.9 0.9 %copy-done.6 = s32[8,64,128]{2,1,0:T(8,128)S(1)} copy-done((s32[8,64,128]{2,1,0:T(8,128)S(1)}, s32[8,64,128]{2,1,0:T(8,128)}, u32[]{:S(2)}) %copy-start.6) | copy-done | bytes 262168
  8.9 0.0 copy-start.7
  8.9 0.7 %copy-done.7 = s32[1,512]{1,0:T(1,128)S(1)} copy-done((s32[1,512]{1,0:T(1,128)S(1)}, s32[1,512]{1,0:T(1,128)}, u32[]{:S(2)}) %copy-start.7) | copy-done | bytes 2072
  9.6 0.0 copy-start.8
  9.6 0.7 %copy-done.8 = f32[6]{0:T(128)S(1)} copy-done((f32[6]{0:T(128)S(1)}, f32[6]{0:T(128)}, u32[]{:S(2)}) %copy-start.8) | copy-done | bytes 48
  10.2 0.0 copy-start.9
  10.2 0.7 %copy-done.9 = f32[6]{0:T(128)S(1)} copy-done((f32[6]{0:T(128)S(1)}, f32[6]{0:T(128)}, u32[]{:S(2)}) %copy-start.9) | copy-done | bytes 48
  10.9 0.0 copy-start.10
  10.9 0.7 %copy-done.10 = s32[1,8]{1,0:T(1,128)S(1)} copy-done((s32[1,8]{1,0:T(1,128)S(1)}, s32[1,8]{1,0:T(1,128)}, u32[]{:S(2)}) %copy-start.10) | copy-done | bytes 56
  11.5 43.6 %shard_map.139 = (f32[1,8,64,128]{3,2,1,0:T(8,128)S(1)}, f32[8,16,128]{2,1,0:T(8,128)S(1)}, f32[8,16,128]{2,1,0:T(8,128)S(1)}) custom-call(f32[1,8,64,128]{3,2,1,0:T(8,128)S(1)} %copy-done.2, f32[1,8,64,128]{3,2,1,0:T(8,128)S(1)} %copy-done.3, f32[1,6,8,64,128]{4,3,2,1,0:T(8,128)S(1)} %copy-done, f32[8,64,128]{2,1,0:T(8,128)S(1)} %copy-done.4, ...), custom_call_target="tpu_custom_call" | custom-call | tf_op jit(solution)/shard_map/pallas_call | solution.py:362
  55.1 0.7 %copy.19 = f32[1,8,64,128]{3,2,1,0:T(8,128)} copy(f32[1,8,64,128]{3,2,1,0:T(8,128)S(1)} %get-tuple-element.6) | data formatting | bytes 524288
  55.8 0.6 %copy.20 = f32[8,16,128]{2,1,0:T(8,128)} copy(f32[8,16,128]{2,1,0:T(8,128)S(1)} %get-tuple-element.7) | data formatting | bytes 131072
  56.5 0.6 %copy.21 = f32[8,16,128]{2,1,0:T(8,128)} copy(f32[8,16,128]{2,1,0:T(8,128)S(1)} %get-tuple-element.8) | data formatting | bytes 131072
Async XLA Ops:
  1.6 1.4 %copy-start = (f32[1,6,8,64,128]{4,3,2,1,0:T(8,128)S(1)}, f32[1,6,8,64,128]{4,3,2,1,0:T(8,128)}, u32[]{:S(2)}) copy-start(f32[1,6,8,64,128]{4,3,2,1,0:T(8,128)} %cost_ref.1) | copy-start | bytes 4718596
  3.0 1.1 %copy-start.1 = (bf16[1,6,8,64,128]{4,3,2,1,0:T(8,128)(2,1)S(1)}, bf16[1,6,8,64,128]{4,3,2,1,0:T(8,128)(2,1)}, u32[]{:S(2)}) copy-start(bf16[1,6,8,64,128]{4,3,2,1,0:T(8,128)(2,1)} %snaps_ref.1) | copy-start | bytes 2359300
  4.1 0.9 %copy-start.2 = (f32[1,8,64,128]{3,2,1,0:T(8,128)S(1)}, f32[1,8,64,128]{3,2,1,0:T(8,128)}, u32[]{:S(2)}) copy-start(f32[1,8,64,128]{3,2,1,0:T(8,128)} %now_ref.1) | copy-start | bytes 786436
  5.1 0.9 %copy-start.3 = (f32[1,8,64,128]{3,2,1,0:T(8,128)S(1)}, f32[1,8,64,128]{3,2,1,0:T(8,128)}, u32[]{:S(2)}) copy-start(f32[1,8,64,128]{3,2,1,0:T(8,128)} %prev_ref.1) | copy-start | bytes 786436
  6.0 0.9 %copy-start.4 = (f32[8,64,128]{2,1,0:T(8,128)S(1)}, f32[8,64,128]{2,1,0:T(8,128)}, u32[]{:S(2)}) copy-start(f32[8,64,128]{2,1,0:T(8,128)} %mod_ref.1) | copy-start | bytes 786436
  7.0 0.9 %copy-start.5 = (f32[8,64,128]{2,1,0:T(8,128)S(1)}, f32[8,64,128]{2,1,0:T(8,128)}, u32[]{:S(2)}) copy-start(f32[8,64,128]{2,1,0:T(8,128)} %relax_ref.1) | copy-start | bytes 786436
  7.9 0.9 %copy-start.6 = (s32[8,64,128]{2,1,0:T(8,128)S(1)}, s32[8,64,128]{2,1,0:T(8,128)}, u32[]{:S(2)}) copy-start(s32[8,64,128]{2,1,0:T(8,128)} %mask_ref.1) | copy-start | bytes 786436
  8.9 0.7 %copy-start.7 = (s32[1,512]{1,0:T(1,128)S(1)}, s32[1,512]{1,0:T(1,128)}, u32[]{:S(2)}) copy-start(s32[1,512]{1,0:T(1,128)} %cells_ref.1) | copy-start | bytes 6148
  9.6 0.7 %copy-start.8 = (f32[6]{0:T(128)S(1)}, f32[6]{0:T(128)}, u32[]{:S(2)}) copy-start(f32[6]{0:T(128)} %rates_ref.1) | copy-start | bytes 76
  10.2 0.7 %copy-start.9 = (f32[6]{0:T(128)S(1)}, f32[6]{0:T(128)}, u32[]{:S(2)}) copy-start(f32[6]{0:T(128)} %weights_ref.1) | copy-start | bytes 76
  10.9 0.7 %copy-start.10 = (s32[1,8]{1,0:T(1,128)S(1)}, s32[1,8]{1,0:T(1,128)}, u32[]{:S(2)}) copy-start(s32[1,8]{1,0:T(1,128)} %signs_ref.1) | copy-start | bytes 100

commit v2 on v1

--- a/solution.py
+++ b/solution.py
@@ -17,18 +17,18 @@
 def kernel(
     shots,
     tiles,
-    now_ref,
-    prev_ref,
-    cost_ref,
-    mod_ref,
-    relax_ref,
-    mask_ref,
+    now_hbm,
+    prev_hbm,
+    cost_hbm,
+    mod_hbm,
+    relax_hbm,
+    mask_hbm,
     rates_ref,
     weights_ref,
-    snaps_ref,
-    cells_ref,
+    snaps_hbm,
+    cells_hbm,
     signs_ref,
-    resid_ref,
+    resid_hbm,
     out_ref,
     own_m_ref,
     own_t_ref,
@@ -49,6 +49,13 @@
     parts,
     low_hot,
     vecs,
+    mod_ref,
+    relax_ref,
+    mask_ref,
+    snaps_ref,
+    cells_ref,
+    resid_ref,
+    loads,
     halo_send,
     halo_recv,
     m_send,
@@ -56,8 +63,8 @@
     t_send,
     t_recv,
 ):
-    steps = snaps_ref.shape[1]
-    mechs = cost_ref.shape[1]
+    steps = snaps_ref.shape[0]
+    mechs = memory.shape[0]
     rows, cols, depth = mod_ref.shape
     half = rows // 2
     wide = cols // CHUNKS
@@ -68,6 +75,25 @@
     tile = lax.axis_index("tile")
     has = (tile > 0, tile < tiles - 1)
     partner = (tile - 1, tile + 1)
+
+    staged = [
+        pltpu.make_async_copy(source, target, loads.at[i])
+        for i, (source, target) in enumerate(
+            (
+                (cost_hbm.at[0], memory),
+                (now_hbm.at[0], adj),
+                (mod_hbm, mod_ref),
+                (relax_hbm, relax_ref),
+                (cells_hbm, cells_ref),
+                (resid_hbm.at[0], resid_ref),
+                (mask_hbm, mask_ref),
+                (prev_hbm.at[0], prev),
+                (snaps_hbm.at[0], snaps_ref),
+            )
+        )
+    ]
+    for load in staged:
+        load.start()
 
     barrier = pltpu.get_barrier_semaphore()
     for side in range(2):
@@ -144,6 +170,9 @@
         vecs[3 * mechs + k - 1] = jnp.where(lane >= k, coeffs[k], 0.0)
         vecs[3 * mechs + 3 + k] = jnp.where(lane < depth - k, coeffs[k], 0.0)
 
+    for load in staged[:4]:
+        load.wait()
+
     def begin(c, carry):
         chunk = chunk_of(c)
         start = pl.multiple_of(chunk * wide, wide)
@@ -151,11 +180,10 @@
         padded = pl.ds(pl.multiple_of(start + PAD, 8), wide)
         total = None
         for m in range(mechs):
-            value = vecs[2 * mechs + m] * cost_ref[0, m, :, at, :]
+            value = vecs[2 * mechs + m] * memory[m, :, at, :]
             memory[m, :, at, :] = value
             total = value if total is None else total + value
-        now = now_ref[0, :, at, :]
-        adj[:, at, :] = now
+        now = adj[:, at, :]
         stress[0, :, padded, :] = mod_ref[:, at, :] * (now - relax_ref[:, at, :] * total)
         return carry
 
@@ -187,9 +215,11 @@
 
     lax.fori_loop(0, steps, clear, 0)
 
+    for load in staged[4:6]:
+        load.wait()
     sources = None
     for e in range(signs_ref.shape[1]):
-        term = signs_ref[0, e].astype(jnp.float32) * resid_ref[0, e]
+        term = signs_ref[0, e].astype(jnp.float32) * resid_ref[:, e]
         sources = term if sources is None else sources + term
     for p in range(3):
         piece = sources.astype(jnp.bfloat16).astype(jnp.float32)
@@ -203,10 +233,12 @@
         lax.broadcasted_iota(jnp.int32, (depth, receivers), 0) == low, 1.0, 0.0
     ).astype(jnp.bfloat16)
 
+    for load in staged[6:]:
+        load.wait()
+
     def prepare(c, carry):
         at = pl.ds(pl.multiple_of(c * wide, wide), wide)
         damp[:, at, :] = 1.0 - damping * mask_ref[:, at, :].astype(jnp.float32)
-        prev[:, at, :] = prev_ref[0, :, at, :]
         grad_m[:, at, :] = jnp.zeros((rows, wide, depth), jnp.float32)
         grad_t[:, at, :] = jnp.zeros((rows, wide, depth), jnp.float32)
         return carry
@@ -249,7 +281,7 @@
             total = value if total is None else total + value
         weighted = mod_ref[:, at, :] * total
         relaxed[:, at, :] = relax_ref[:, at, :] * weighted
-        gained = grad_t[:, at, :] + weighted * snaps_ref[0, steps - 1 - k, :, at, :].astype(jnp.float32)
+        gained = grad_t[:, at, :] + weighted * snaps_ref[steps - 1 - k, :, at, :].astype(jnp.float32)
         if last:
             for i in range(per):
                 owner = chunk * per + i
@@ -279,7 +311,7 @@
                 term = coeffs[j] * shifted
                 extra = term if extra is None else extra + term
             fresh = base[lines, at, :] + damp[lines, at, :] * extra
-            gained = grad_m[lines, at, :] + fresh * snaps_ref[0, steps - 1 - k, lines, at, :].astype(jnp.float32)
+            gained = grad_m[lines, at, :] + fresh * snaps_ref[steps - 1 - k, lines, at, :].astype(jnp.float32)
             if last:
                 out_ref[0, lines, at, :] = fresh
                 for i in range(per):
@@ -349,7 +381,8 @@
     tiles = mesh.shape["tile"]
 
     def shards(*args):
-        now, _, costates, modulus, _, _, _, _, snaps, cells, _, _ = args
+        now, _, costates, modulus, _, _, _, _, snaps, cells, _, resid = args
+        resid = jnp.transpose(resid, (0, 2, 1, 3))
         rows, cols, depth = modulus.shape
         mechs = costates.shape[1]
         steps = snaps.shape[1]
@@ -358,6 +391,7 @@
         field = pltpu.VMEM((rows, cols, depth), jnp.float32)
         blocks = pltpu.VMEM((shots, rows, owned, depth), jnp.float32)
         vmem = pl.BlockSpec(memory_space=pltpu.VMEM)
+        hbm = pl.BlockSpec(memory_space=pltpu.HBM)
         smem = pl.BlockSpec(memory_space=pltpu.SMEM)
         return pl.pallas_call(
             functools.partial(kernel, shots, tiles),
@@ -366,7 +400,7 @@
                 jax.ShapeDtypeStruct((rows, owned, depth), jnp.float32),
                 jax.ShapeDtypeStruct((rows, owned, depth), jnp.float32),
             ),
-            in_specs=[vmem] * 6 + [smem] * 2 + [vmem] * 2 + [smem, vmem],
+            in_specs=[hbm] * 6 + [smem] * 2 + [hbm] * 2 + [smem, hbm],
             out_specs=(vmem, vmem, vmem),
             scratch_shapes=[
                 pltpu.VMEM((steps, rows, cols + 2 * PAD, depth), jnp.float32),
@@ -386,6 +420,13 @@
                 pltpu.VMEM((steps, 8, receivers), jnp.float32),
                 pltpu.VMEM((depth, receivers), jnp.bfloat16),
                 pltpu.VMEM((3 * mechs + 8, 1, depth), jnp.float32),
+                field,
+                field,
+                pltpu.VMEM((rows, cols, depth), jnp.int32),
+                pltpu.VMEM(snaps.shape[1:], snaps.dtype),
+                pltpu.VMEM(cells.shape, cells.dtype),
+                pltpu.VMEM(resid.shape[1:], resid.dtype),
+                pltpu.SemaphoreType.DMA((9,)),
                 pltpu.SemaphoreType.DMA((steps, 2, CHUNKS)),
                 pltpu.SemaphoreType.DMA((steps, 2, CHUNKS)),
                 pltpu.SemaphoreType.DMA((shots, 2)),
@@ -394,9 +435,9 @@
                 pltpu.SemaphoreType.DMA((shots,)),
             ],
             compiler_params=pltpu.CompilerParams(
-                collective_id=0, has_side_effects=True, vmem_limit_bytes=40 * 1024 * 1024
+                collective_id=0, has_side_effects=True, vmem_limit_bytes=63 * 1024 * 1024
             ),
-        )(*args)
+        )(*args[:-1], resid)
 
     return jax.shard_map(
         shards,

time: 57.5 us -> 50.7 us (0.88)
  local copies, waits for them, and re-layouts: 12.8 us -> 4.62 us
  Pallas kernels: 43.6 us -> 45.2 us
    unnamed x26 -> x3, local copies, waits for them, and re-layouts: 12.8 us -> 4.62 us
    pallas_call x1, Pallas kernels: 43.6 us -> 45.2 us  [shards(): pl.pallas_call(functools.partial(kernel, shots, tiles), out_shape=(jax.Sh...]
where the time goes in v2:
time: 50.7 us; the launch traced here: 50.5 us
  Pallas kernels  45.2 us (89%)
  local copies, waits for them, and re-layouts  4.62 us (9%)
  between operations  0.64 us (1%)
    pallas_call x1, Pallas kernels, shards(): pl.pallas_call(functools.partial(kernel, shots, tiles), out_shape=(jax.Sh...  45.2 us
    unnamed x3, local copies, waits for them, and re-layouts  4.62 us

profile of v2, /device:TPU:9, one launch (start us, length us, event | category | flops | bytes accessed | tf_op | source)
XLA Modules:
  0.0 50.5 jit_solution(5658664486646025492)
XLA Ops:
  0.6 45.2 %shard_map.139 = (f32[1,8,64,128]{3,2,1,0:T(8,128)}, f32[8,16,128]{2,1,0:T(8,128)}, f32[8,16,128]{2,1,0:T(8,128)}) custom-call(f32[1,8,64,128]{3,2,1,0:T(8,128)} %now_hbm.1, f32[1,8,64,128]{3,2,1,0:T(8,128)} %prev_hbm.1, f32[1,6,8,64,128]{4,3,2,1,0:T(8,128)} %cost_hbm.1, f32[8,64,128]{2,1,0:T(8,128)} %mod_hbm.1, f32[8,64,128]{2,1,0:T(8,128)} %relax_hbm.1, ...), custom_call_target="tpu_custom_call" | custom-call | tf_op jit(solution)/shard_map/pallas_call | solution.py:396
  45.9 1.7 %copy.18 = f32[1,8,64,128]{3,2,1,0:T(8,128)} copy(f32[1,8,64,128]{3,2,1,0:T(8,128)} %get-tuple-element.6) | data formatting | bytes 524288
  47.5 1.5 %copy.19 = f32[8,16,128]{2,1,0:T(8,128)} copy(f32[8,16,128]{2,1,0:T(8,128)} %get-tuple-element.7) | data formatting | bytes 131072
  49.0 1.5 %copy.20 = f32[8,16,128]{2,1,0:T(8,128)} copy(f32[8,16,128]{2,1,0:T(8,128)} %get-tuple-element.8) | data formatting | bytes 131072

commit v3 on v2

--- a/solution.py
+++ b/solution.py
@@ -55,6 +55,7 @@
     snaps_ref,
     cells_ref,
     resid_ref,
+    early_loads,
     loads,
     halo_send,
     halo_recv,
@@ -76,14 +77,34 @@
     has = (tile > 0, tile < tiles - 1)
     partner = (tile - 1, tile + 1)
 
+    first = lax.rem(me // per + 1, CHUNKS)
+
+    def chunk_of(c):
+        return lax.rem(first + c, CHUNKS)
+
+    def early(c):
+        start = pl.multiple_of(chunk_of(c) * wide, wide)
+        at = pl.ds(start, wide)
+        return [
+            pltpu.make_async_copy(source, target, early_loads.at[c, i])
+            for i, (source, target) in enumerate(
+                (
+                    (cost_hbm.at[0, :, :, at, :], memory.at[:, :, at, :]),
+                    (now_hbm.at[0, :, at, :], adj.at[:, at, :]),
+                    (mod_hbm.at[:, at, :], mod_ref.at[:, at, :]),
+                    (relax_hbm.at[:, at, :], relax_ref.at[:, at, :]),
+                )
+            )
+        ]
+
+    for c in range(CHUNKS):
+        for load in early(c):
+            load.start()
+
     staged = [
         pltpu.make_async_copy(source, target, loads.at[i])
         for i, (source, target) in enumerate(
             (
-                (cost_hbm.at[0], memory),
-                (now_hbm.at[0], adj),
-                (mod_hbm, mod_ref),
-                (relax_hbm, relax_ref),
                 (cells_hbm, cells_ref),
                 (resid_hbm.at[0], resid_ref),
                 (mask_hbm, mask_ref),
@@ -154,11 +175,6 @@
             device_id_type=MESH,
         )
 
-    first = lax.rem(me // per + 1, CHUNKS)
-
-    def chunk_of(c):
-        return lax.rem(first + c, CHUNKS)
-
     for m in range(mechs):
         decay = jnp.exp(jnp.full((1, depth), -rates_ref[m], jnp.float32))
         weight = jnp.full((1, depth), weights_ref[m], jnp.float32)
@@ -170,14 +186,19 @@
         vecs[3 * mechs + k - 1] = jnp.where(lane >= k, coeffs[k], 0.0)
         vecs[3 * mechs + 3 + k] = jnp.where(lane < depth - k, coeffs[k], 0.0)
 
-    for load in staged[:4]:
-        load.wait()
+    def begin_send(c, carry):
+        start = pl.multiple_of(chunk_of(c) * wide, wide)
+        for side in range(2):
+            send_halo(0, side, start)
+        return carry
 
     def begin(c, carry):
         chunk = chunk_of(c)
         start = pl.multiple_of(chunk * wide, wide)
         at = pl.ds(start, wide)
         padded = pl.ds(pl.multiple_of(start + PAD, 8), wide)
+        for load in early(c):
+            load.wait()
         total = None
         for m in range(mechs):
             value = vecs[2 * mechs + m] * memory[m, :, at, :]
@@ -187,18 +208,16 @@
         stress[0, :, padded, :] = mod_ref[:, at, :] * (now - relax_ref[:, at, :] * total)
         return carry
 
-    lax.fori_loop(0, CHUNKS, begin, 0)
-
+    begin(0, 0)
     peers = shots - 1 + has[0].astype(jnp.int32) + has[1].astype(jnp.int32)
     pl.semaphore_wait(barrier, peers)
-
-    def begin_send(c, carry):
-        start = pl.multiple_of(chunk_of(c) * wide, wide)
-        for side in range(2):
-            send_halo(0, side, start)
-        return carry
-
-    lax.fori_loop(0, CHUNKS, begin_send, 0)
+    begin_send(0, 0)
+
+    def begin_both(c, carry):
+        begin(c, carry)
+        return begin_send(c, carry)
+
+    lax.fori_loop(1, CHUNKS, begin_both, 0)
 
     empty = jnp.zeros((rows, PAD, depth), jnp.float32)
 
@@ -215,7 +234,7 @@
 
     lax.fori_loop(0, steps, clear, 0)
 
-    for load in staged[4:6]:
+    for load in staged[:2]:
         load.wait()
     sources = None
     for e in range(signs_ref.shape[1]):
@@ -233,7 +252,7 @@
         lax.broadcasted_iota(jnp.int32, (depth, receivers), 0) == low, 1.0, 0.0
     ).astype(jnp.bfloat16)
 
-    for load in staged[6:]:
+    for load in staged[2:]:
         load.wait()
 
     def prepare(c, carry):
@@ -245,7 +264,7 @@
 
     lax.fori_loop(0, CHUNKS, prepare, 0)
 
-    def before(k, c, last):
+    def local(k, c, last):
         chunk = chunk_of(c)
         start = pl.multiple_of(chunk * wide, wide)
         at = pl.ds(start, wide)
@@ -260,19 +279,8 @@
             )
             inject = term if inject is None else inject + term
         inject = inject.reshape(rows, wide, depth)
-        window = stress[k, :, pl.ds(start, wide + 2 * PAD), :]
-        center = window[:, PAD : PAD + wide]
-        zeros = jnp.zeros((4, wide, depth), jnp.float32)
-        tall = jnp.concatenate([zeros, center, zeros], axis=0)
-        lap = (3.0 * coeffs[0]) * center
-        for j in range(1, 5):
-            near = window[:, PAD + j : PAD + j + wide] + window[:, PAD - j : PAD - j + wide]
-            near = near + (tall[4 + j : 4 + j + rows] + tall[4 - j : 4 - j + rows])
-            lap = lap + coeffs[j] * near
-            lap = lap + vecs[3 * mechs + j - 1] * pltpu.roll(center, j, 2)
-            lap = lap + vecs[3 * mechs + 3 + j] * pltpu.roll(center, depth - j, 2)
         now = adj[:, at, :]
-        base[:, at, :] = damp[:, at, :] * (2.0 * now - prev[:, at, :] + lap + inject)
+        base[:, at, :] = 2.0 * now - prev[:, at, :] + inject
         prev[:, at, :] = now
         total = None
         for m in range(mechs):
@@ -292,6 +300,22 @@
                     t_copy(owner, me).start()
         else:
             grad_t[:, at, :] = gained
+
+    def across(k, c):
+        start = pl.multiple_of(chunk_of(c) * wide, wide)
+        at = pl.ds(start, wide)
+        window = stress[k, :, pl.ds(start, wide + 2 * PAD), :]
+        center = window[:, PAD : PAD + wide]
+        zeros = jnp.zeros((4, wide, depth), jnp.float32)
+        tall = jnp.concatenate([zeros, center, zeros], axis=0)
+        lap = (3.0 * coeffs[0]) * center
+        for j in range(1, 5):
+            near = window[:, PAD + j : PAD + j + wide] + window[:, PAD - j : PAD - j + wide]
+            near = near + (tall[4 + j : 4 + j + rows] + tall[4 - j : 4 - j + rows])
+            lap = lap + coeffs[j] * near
+            lap = lap + vecs[3 * mechs + j - 1] * pltpu.roll(center, j, 2)
+            lap = lap + vecs[3 * mechs + 3 + j] * pltpu.roll(center, depth - j, 2)
+        base[:, at, :] = damp[:, at, :] * (base[:, at, :] + lap)
 
     def after(k, c, last):
         chunk = chunk_of(c)
@@ -328,21 +352,43 @@
                 adj[lines, at, :] = fresh
                 grad_m[lines, at, :] = gained
 
-    def loop(k, body, last):
+    def each(body):
         def one(c, carry):
-            body(k, c, last)
+            body(c)
             return carry
 
         lax.fori_loop(0, CHUNKS, one, 0)
 
-    def step(k, carry):
-        loop(k, before, False)
-        loop(k, after, False)
+    def step(k, last):
+        def one(c):
+            after(k, c, False)
+            local(k + 1, c, last)
+
+        each(one)
+        each(lambda c: across(k + 1, c))
+
+    each(lambda c: local(0, c, False))
+    each(lambda c: across(0, c))
+
+    def middle(k, carry):
+        step(k, False)
         return carry
 
-    lax.fori_loop(0, steps - 1, step, 0)
-    loop(steps - 1, before, True)
-    loop(steps - 1, after, True)
+    lax.fori_loop(0, steps - 2, middle, 0)
+    step(steps - 2, True)
+
+    def finish(k, carry):
+        for side in range(2):
+            for c in range(CHUNKS):
+
+                @pl.when(has[side])
+                def _():
+                    halo_copy(k, side, c * wide).wait_send()
+
+        return carry
+
+    lax.fori_loop(0, steps - 1, finish, 0)
+    each(lambda c: after(steps - 1, c, True))
 
     total_t = send_t[me]
     for away in range(1, shots):
@@ -358,22 +404,23 @@
         total_m = total_m + got_m[source]
     own_m_ref[...] = total_m
 
-    def finish(k, carry):
-        for side in range(2):
-            for c in range(CHUNKS):
-
-                @pl.when(has[side])
-                def _():
-                    halo_copy(k, side, c * wide).wait_send()
-
-        return carry
-
-    lax.fori_loop(0, steps, finish, 0)
+    finish(steps - 1, 0)
     for away in range(1, shots):
         owner = lax.rem(me + away, shots)
         t_copy(owner, me).wait_send()
         for side in range(2):
             m_copy(owner, me, side).wait_send()
+
+
+def store(a, b, c, to_a, to_b, to_c, sems):
+    copies = [
+        pltpu.make_async_copy(source, target, sems.at[i])
+        for i, (source, target) in enumerate(((a, to_a), (b, to_b), (c, to_c)))
+    ]
+    for copy in copies:
+        copy.start()
+    for copy in copies:
+        copy.wait()
 
 
 def solution(mesh):
@@ -393,12 +440,12 @@
         vmem = pl.BlockSpec(memory_space=pltpu.VMEM)
         hbm = pl.BlockSpec(memory_space=pltpu.HBM)
         smem = pl.BlockSpec(memory_space=pltpu.SMEM)
-        return pl.pallas_call(
+        results = pl.pallas_call(
             functools.partial(kernel, shots, tiles),
             out_shape=(
-                jax.ShapeDtypeStruct(now.shape, jnp.float32),
-                jax.ShapeDtypeStruct((rows, owned, depth), jnp.float32),
-                jax.ShapeDtypeStruct((rows, owned, depth), jnp.float32),
+                pltpu.VMEM(now.shape, jnp.float32),
+                pltpu.VMEM((rows, owned, depth), jnp.float32),
+                pltpu.VMEM((rows, owned, depth), jnp.float32),
             ),
             in_specs=[hbm] * 6 + [smem] * 2 + [hbm] * 2 + [smem, hbm],
             out_specs=(vmem, vmem, vmem),
@@ -426,7 +473,8 @@
                 pltpu.VMEM(snaps.shape[1:], snaps.dtype),
                 pltpu.VMEM(cells.shape, cells.dtype),
                 pltpu.VMEM(resid.shape[1:], resid.dtype),
-                pltpu.SemaphoreType.DMA((9,)),
+                pltpu.SemaphoreType.DMA((CHUNKS, 4)),
+                pltpu.SemaphoreType.DMA((5,)),
                 pltpu.SemaphoreType.DMA((steps, 2, CHUNKS)),
                 pltpu.SemaphoreType.DMA((steps, 2, CHUNKS)),
                 pltpu.SemaphoreType.DMA((shots, 2)),
@@ -438,6 +486,13 @@
                 collective_id=0, has_side_effects=True, vmem_limit_bytes=63 * 1024 * 1024
             ),
         )(*args[:-1], resid)
+        return pl.pallas_call(
+            store,
+            out_shape=[jax.ShapeDtypeStruct(r.shape, r.dtype) for r in results],
+            in_specs=[vmem] * 3,
+            out_specs=[pl.BlockSpec(memory_space=pl.ANY)] * 3,
+            scratch_shapes=[pltpu.SemaphoreType.DMA((3,))],
+        )(*[pltpu.with_memory_space_constraint(r, pltpu.VMEM) for r in results])
 
     return jax.shard_map(
         shards,

time: 50.7 us -> 44 us (0.87)
  local copies, waits for them, and re-layouts: 4.62 us -> 0 us
  Pallas kernels: 45.2 us -> 42.8 us
    unnamed x3 -> x0, local copies, waits for them, and re-layouts: 4.62 us -> none
    pallas_call x1 -> x2, Pallas kernels: 45.2 us -> 42.8 us  [the longest x1 42 us: shards(): pl.pallas_call(functools.partial(kernel, shots, tiles), out_shape=(pltpu....]
where the time goes in v3:
time: 44 us; the launch traced here: 43.4 us
  Pallas kernels  42.8 us (97%)
  between operations  0.64 us (1%)
    pallas_call x1, Pallas kernels, shards(): pl.pallas_call(functools.partial(kernel, shots, tiles), out_shape=(pltpu....  42 us

profile of v3, /device:TPU:9, one launch (start us, length us, event | category | flops | bytes accessed | tf_op | source)
XLA Modules:
  0.0 43.4 jit_solution(16668840418724966992)
XLA Ops:
  0.6 42.0 %shard_map.139 = (f32[1,8,64,128]{3,2,1,0:T(8,128)S(1)}, f32[8,16,128]{2,1,0:T(8,128)S(1)}, f32[8,16,128]{2,1,0:T(8,128)S(1)}) custom-call(f32[1,8,64,128]{3,2,1,0:T(8,128)} %now_hbm.1, f32[1,8,64,128]{3,2,1,0:T(8,128)} %prev_hbm.1, f32[1,6,8,64,128]{4,3,2,1,0:T(8,128)} %cost_hbm.1, f32[8,64,128]{2,1,0:T(8,128)} %mod_hbm.1, f32[8,64,128]{2,1,0:T(8,128)} %relax_hbm.1, ...), custom_call_target="tpu_custom_call" | custom-call | tf_op jit(solution)/shard_map/pallas_call | solution.py:443
  42.7 0.8 %shard_map.140 = (f32[1,8,64,128]{3,2,1,0:T(8,128)}, f32[8,16,128]{2,1,0:T(8,128)}, f32[8,16,128]{2,1,0:T(8,128)}) custom-call(f32[1,8,64,128]{3,2,1,0:T(8,128)S(1)} %get-tuple-element.6.a, f32[8,16,128]{2,1,0:T(8,128)S(1)} %get-tuple-element.7.b, f32[8,16,128]{2,1,0:T(8,128)S(1)} %get-tuple-element.8.c), custom_call_target="tpu_custom_call" | custom-call | tf_op jit(solution)/shard_map/pallas_call | solution.py:489

commit v4 on v3

--- a/solution.py
+++ b/solution.py
@@ -388,14 +388,19 @@
         return carry
 
     lax.fori_loop(0, steps - 1, finish, 0)
-    each(lambda c: after(steps - 1, c, True))
-
+    def closing(c, carry):
+        after(steps - 1, c, True)
+        return carry
+
+    lax.fori_loop(0, CHUNKS - 1, closing, 0)
     total_t = send_t[me]
     for away in range(1, shots):
         source = lax.rem(me + away, shots)
         t_copy(source, source).wait_recv()
         total_t = total_t + got_t[source]
     own_t_ref[...] = total_t
+    after(steps - 1, CHUNKS - 1, True)
+
     total_m = send_m[me]
     for away in range(1, shots):
         source = lax.rem(me + away, shots)

time: 44 us -> 44 us (level)
  no operation moved by 1% of the time
where the time goes in v4:
time: 44 us; the launch traced here: 43.4 us
  Pallas kernels  42.8 us (97%)
  between operations  0.64 us (1%)
    pallas_call x1, Pallas kernels, shards(): pl.pallas_call(functools.partial(kernel, shots, tiles), out_shape=(pltpu....  42 us

profile of v4, /device:TPU:9, one launch (start us, length us, event | category | flops | bytes accessed | tf_op | source)
XLA Modules:
  0.0 43.4 jit_solution(691964641009887600)
XLA Ops:
  0.6 42.0 %shard_map.139 = (f32[1,8,64,128]{3,2,1,0:T(8,128)S(1)}, f32[8,16,128]{2,1,0:T(8,128)S(1)}, f32[8,16,128]{2,1,0:T(8,128)S(1)}) custom-call(f32[1,8,64,128]{3,2,1,0:T(8,128)} %now_hbm.1, f32[1,8,64,128]{3,2,1,0:T(8,128)} %prev_hbm.1, f32[1,6,8,64,128]{4,3,2,1,0:T(8,128)} %cost_hbm.1, f32[8,64,128]{2,1,0:T(8,128)} %mod_hbm.1, f32[8,64,128]{2,1,0:T(8,128)} %relax_hbm.1, ...), custom_call_target="tpu_custom_call" | custom-call | tf_op jit(solution)/shard_map/pallas_call | solution.py:448
  42.7 0.8 %shard_map.140 = (f32[1,8,64,128]{3,2,1,0:T(8,128)}, f32[8,16,128]{2,1,0:T(8,128)}, f32[8,16,128]{2,1,0:T(8,128)}) custom-call(f32[1,8,64,128]{3,2,1,0:T(8,128)S(1)} %get-tuple-element.6.a, f32[8,16,128]{2,1,0:T(8,128)S(1)} %get-tuple-element.7.b, f32[8,16,128]{2,1,0:T(8,128)S(1)} %get-tuple-element.8.c), custom_call_target="tpu_custom_call" | custom-call | tf_op jit(solution)/shard_map/pallas_call | solution.py:494
